TPU v7x, 32 devices: a whole 2x2x4 slice. The times are simulated.
32 devices in a mesh: groups: 2 (over y), seq: 4 (over z), strand: 2 (over core), chan: 2 (over x).
Axes of the slice: x: 2, y: 2, z: 4, core: 2. Of those that a mesh axis runs over, the one named last changes fastest.
Arguments:
- seq_in: bfloat16 [2, 6144, 512], P('strand', ('groups', 'seq', 'chan')), parts along dimension 1, may hold values from -6 to 6
- conv_norm: float32 [2, 512], replicated, may hold values from 0.1 to 1.9
- conv_weight: bfloat16 [2, 3, 512, 512], P(None, None, None, ('seq', 'chan')), may hold values from -0.15625 to 0.15625
- ff_norm: float32 [2, 512], replicated, may hold values from 0.1 to 1.9
- up_weight: bfloat16 [2, 512, 2048], P(None, None, ('seq', 'chan')), may hold values from -0.25 to 0.25
- down_weight: bfloat16 [2, 2048, 512], P(None, ('seq', 'chan')), may hold values from -0.125 to 0.125
- head_norm: float32 [512], replicated, may hold values from 0.1 to 1.9
- value_weight: bfloat16 [512, 512], replicated, may hold values from -0.25 to 0.25
- gate_weight: bfloat16 [512, 512], replicated, may hold values from -0.25 to 0.25
- out_weight: bfloat16 [512, 512], replicated, may hold values from -0.25 to 0.25
Outputs:
- strand_out: bfloat16 [2, 6144, 512], P('strand', ('groups', 'seq', 'chan')), parts along dimension 1
There are 2 independent parts, one for each index of `groups`. A program takes and returns all parts, laid end to end along the dimension named above; an argument that names none is the same for every part. Nothing has to cross between parts.
All inputs are finite; a program needn't handle non-finite values.
Results may differ from a plain program's by a relative error of at most 0.015.
Values may be sent and summed in bfloat16 or wider, within the bound.
No kernel may reach another device: no remote copies, remote signals or barrier semaphores. Data moves between devices by JAX's collectives and lax.ppermute only.
A program may use at most 64 MiB of HBM per device.

v0:
```python
import jax
import jax.numpy as jnp
from jax import lax
from jax.sharding import PartitionSpec as P


def passed_along(value, axis, steps):
    count = lax.axis_size(axis)
    initial, last = (max(0, -steps), min(count, count - steps))
    return lax.ppermute(value, axis, [(source, source + steps) for source in range(initial, last)])


def swapped(x, axis, stride):
    return lax.ppermute(x, axis, [(i, i ^ 1 << stride) for i in range(lax.axis_size(axis))])


def normalize(values, gain):
    return values * lax.rsqrt(jnp.mean(values * values, axis=-1, keepdims=True) + 1e-06) * gain


def matmul(left, right):
    return jnp.dot(left, right, preferred_element_type=jnp.float32)


def local(
    seq_in,
    conv_norm,
    conv_weight,
    ff_norm,
    up_weight,
    down_weight,
    head_norm,
    value_weight,
    gate_weight,
    out_weight,
):
    state = seq_in[0].astype(jnp.float32)
    seq_count = lax.axis_size("seq")
    for block in range(conv_weight.shape[0]):
        reach = min(2**block, seq_count // 2)
        normed = normalize(state, conv_norm[block]).astype(jnp.bfloat16)
        before = passed_along(normed, "seq", reach)
        after = passed_along(normed, "seq", -reach)
        piece = lax.all_gather(conv_weight[block], ("seq", "chan"), axis=2, tiled=True)
        total = matmul(before, piece[0]) + matmul(normed, piece[1]) + matmul(after, piece[2])
        conv = total.astype(jnp.bfloat16)
        state = state + conv.astype(jnp.float32)
        mixed = normalize(state, ff_norm[block]).astype(jnp.bfloat16)
        hidden = jax.nn.gelu(
            matmul(mixed, lax.all_gather(up_weight[block], ("seq", "chan"), axis=1, tiled=True))
        ).astype(jnp.bfloat16)
        state = state + matmul(
            hidden, lax.all_gather(down_weight[block], ("seq", "chan"), axis=0, tiled=True)
        )
    final = normalize(state, head_norm).astype(jnp.bfloat16)
    value = matmul(final, value_weight)
    bit_count = (seq_count * lax.axis_size("chan")).bit_length() - 1
    opposite = swapped(final, "strand", 0)
    for digit in range(bit_count):
        opposite = swapped(opposite, ("seq", "chan"), digit)
    opposite = jnp.flip(opposite, 0)
    mirrored = matmul(opposite, gate_weight).astype(jnp.bfloat16)
    gated = (value * jax.nn.sigmoid(mirrored.astype(jnp.float32))).astype(jnp.bfloat16)
    result = matmul(gated, out_weight)
    return result.astype(jnp.bfloat16)[None]


def solution(mesh):
    in_specs = (
        P("strand", ("groups", "seq", "chan"), None),
        P(),
        P(None, None, None, ("seq", "chan")),
        P(),
        P(None, None, ("seq", "chan")),
        P(None, ("seq", "chan"), None),
        P(),
        P(),
        P(),
        P(),
    )
    out_specs = P("strand", ("groups", "seq", "chan"), None)
    return jax.shard_map(local, mesh=mesh, in_specs=in_specs, out_specs=out_specs, check_vma=False)
```

profile of v0, /device:TPU:0, one launch (start us, length us, event | category | flops | bytes accessed | tf_op | source)
XLA Modules:
  0.0 376.3 jit_solution(10085259237027235437)
XLA Ops:
  6.5 0.0 all-gather.13.cloned.1.call-start
  6.6 1.9 fusion.86
  8.5 0.0 all-gather.15.cloned.1.call-start
  8.6 1.9 fusion.84
  10.5 0.0 all-gather.17.cloned.1.call-start
  10.5 0.8 fusion.85
  11.4 0.0 all-gather.19.cloned.1.call-start
  11.4 0.5 all-gather.19.cloned.1.call-update
  12.0 0.0 all-gather.21.cloned.1.call-start
  12.0 0.5 all-gather.21.cloned.1.call-update
  12.6 0.0 all-gather.23.cloned.1.call-start
  12.6 0.2 fusion.55
  12.8 0.2 fusion.57
  13.0 1.3 collective-permute-start.1
  14.3 0.0 all-gather.23.cloned.1.call-update
  14.3 5.6 %collective-permute-start = (bf16[384,512]{1,0:T(8,128)(2,1)S(1)}, bf16[384,512]{1,0:T(8,128)(2,1)S(1)}, u32[]{:S(2)}, u32[]{:S(2)}) collective-permute-start(bf16[384,512]{1,0:T(8,128)(2,1)S(1)} %fusion.57), channel_id=1, source_target_pairs={{0,4},{4,8},{8,12},{1,5},{5,9},{9,13},{2,6},{6,10},{10,14},{3,7},{... | collective-permute-start | bytes 1179656 | tf_op jit(solution)/shard_map/ppermute | solution.py:10
  19.9 10.7 %collective-permute-done.1 = bf16[384,512]{1,0:T(8,128)(2,1)S(1)} collective-permute-done((bf16[384,512]{1,0:T(8,128)(2,1)S(1)}, bf16[384,512]{1,0:T(8,128)(2,1)S(1)}, u32[]{:S(2)}, u32[]{:S(2)}) %collective-permute-start.1) | collective-permute-done | bytes 393248 | tf_op jit(solution)/shard_map/ppermute | solution.py:10
  30.6 28.5 %all-gather.13.cloned.1.call-done = bf16[1,3,512,512]{2,3,1,0:T(8,128)(2,1)} async-done(((bf16[1,3,512,64]{2,3,1,0:T(8,128)(2,1)}), bf16[1,3,512,512]{2,3,1,0:T(8,128)(2,1)}) %all-gather.13.cloned.1.call-update) | async-done | bytes 1572880 | tf_op jit(solution)/shard_map/all_gather | solution.py:44
  59.0 1.4 fusion.62
  60.5 1.5 fusion.63
  62.0 1.6 multiply_reduce_fusion.3
  63.6 47.5 %all-gather.15.cloned.1.call-done = bf16[1,512,2048]{2,1,0:T(8,128)(2,1)} async-done(((bf16[1,512,256]{2,1,0:T(8,128)(2,1)}), bf16[1,512,2048]{2,1,0:T(8,128)(2,1)}) %all-gather.15.cloned.1.call-update) | async-done | bytes 2097168 | tf_op jit(solution)/shard_map/all_gather | solution.py:50
  111.0 49.6 %all-gather.17.cloned.1.call-done = bf16[1,2048,512]{2,1,0:T(8,128)(2,1)} async-done(((bf16[1,256,512]{2,1,0:T(8,128)(2,1)}), bf16[1,2048,512]{2,1,0:T(8,128)(2,1)}) %all-gather.17.cloned.1.call-update) | async-done | bytes 2097168 | tf_op jit(solution)/shard_map/all_gather | solution.py:53
  160.7 4.4 %multiply_reduce_fusion.2 = (f32[384]{0:T(512)S(1)}, f32[384,512]{1,0:T(8,128)S(1)}) fusion(f32[384,512]{1,0:T(8,128)S(1)} %get-tuple-element.16, bf16[1,2048,512]{2,1,0:T(8,128)(2,1)} %all-gather.17.cloned.1.call-done, bf16[1,512,2048]{2,1,0:T(8,128)(2,1)} %all-gather.15.cloned.1.call-done, f32[512]{0:T(512)S(1)} %bitcast.91, f32[384]{0:T(512)S(1)} %add_rsqrt_fusion.3), kind=kOutput, calls=%fused_computation.62 | convolution fusion | flops 1618869888 | bytes 5772288 | tf_op jit(solution)/shard_map/dot_general | solution.py:22
  165.0 0.1 multiply_convert_fusion.4
  165.2 1.3 collective-permute-start.3
  166.5 5.5 %collective-permute-start.2 = (bf16[384,512]{1,0:T(8,128)(2,1)S(1)}, bf16[384,512]{1,0:T(8,128)(2,1)S(1)}, u32[]{:S(2)}, u32[]{:S(2)}) collective-permute-start(bf16[384,512]{1,0:T(8,128)(2,1)S(1)} %multiply_convert_fusion.4), channel_id=1, source_target_pairs={{0,8},{4,12},{1,9},{5,13},{2,10},{6,14},{3,11},{7,15},{16,24},{20,... | collective-permute-start | bytes 1179656 | tf_op jit(solution)/shard_map/ppermute | solution.py:10
  172.0 46.6 %all-gather.19.cloned.1.call-done = bf16[1,3,512,512]{2,3,1,0:T(8,128)(2,1)} async-done(((bf16[1,3,512,64]{2,3,1,0:T(8,128)(2,1)}), bf16[1,3,512,512]{2,3,1,0:T(8,128)(2,1)}) %all-gather.19.cloned.1.call-update) | async-done | bytes 1572880 | tf_op jit(solution)/shard_map/all_gather | solution.py:44
  218.6 1.4 fusion.61
  220.1 1.4 fusion.60
  221.5 1.6 multiply_reduce_fusion.1
  223.1 47.3 %all-gather.21.cloned.1.call-done = bf16[1,512,2048]{2,1,0:T(8,128)(2,1)} async-done(((bf16[1,512,256]{2,1,0:T(8,128)(2,1)}), bf16[1,512,2048]{2,1,0:T(8,128)(2,1)}) %all-gather.21.cloned.1.call-update) | async-done | bytes 2097168 | tf_op jit(solution)/shard_map/all_gather | solution.py:50
  270.4 49.5 %all-gather.23.cloned.1.call-done = bf16[1,2048,512]{2,1,0:T(8,128)(2,1)} async-done(((bf16[1,256,512]{2,1,0:T(8,128)(2,1)}), bf16[1,2048,512]{2,1,0:T(8,128)(2,1)}) %all-gather.23.cloned.1.call-update) | async-done | bytes 2097168 | tf_op jit(solution)/shard_map/all_gather | solution.py:53
  319.9 4.4 %multiply_reduce_fusion = (f32[384]{0:T(512)S(1)}, f32[384,512]{1,0:T(8,128)S(1)}) fusion(f32[384,512]{1,0:T(8,128)S(1)} %get-tuple-element.20, bf16[1,2048,512]{2,1,0:T(8,128)(2,1)} %all-gather.23.cloned.1.call-done, bf16[1,512,2048]{2,1,0:T(8,128)(2,1)} %all-gather.21.cloned.1.call-done, f32[512]{0:T(512)S(1)} %bitcast.90, f32[384]{0:T(512)S(1)} %add_rsqrt_fusion.1), kind=kOutput, calls=%fused_computation.58 | convolution fusion | flops 1618869888 | bytes 5772288 | tf_op jit(solution)/shard_map/dot_general | solution.py:22
  324.3 0.1 multiply_convert_fusion
  324.4 0.1 collective-permute-start.4
  324.5 1.7 collective-permute-done.4
  326.2 0.6 collective-permute-start.5
  326.8 10.6 %collective-permute-done.5 = bf16[384,512]{1,0:T(8,128)(2,1)S(1)} collective-permute-done((bf16[384,512]{1,0:T(8,128)(2,1)S(1)}, bf16[384,512]{1,0:T(8,128)(2,1)S(1)}, u32[]{:S(2)}, u32[]{:S(2)}) %collective-permute-start.5) | collective-permute-done | bytes 393248 | tf_op jit(solution)/shard_map/ppermute | solution.py:14
  337.4 1.5 collective-permute-start.6
  338.8 8.8 %collective-permute-done.6 = bf16[384,512]{1,0:T(8,128)(2,1)S(1)} collective-permute-done((bf16[384,512]{1,0:T(8,128)(2,1)S(1)}, bf16[384,512]{1,0:T(8,128)(2,1)S(1)}, u32[]{:S(2)}, u32[]{:S(2)}) %collective-permute-start.6) | collective-permute-done | bytes 393248 | tf_op jit(solution)/shard_map/ppermute | solution.py:14
  347.7 1.8 collective-permute-start.7
  349.5 16.9 %collective-permute-done.7 = bf16[384,512]{1,0:T(8,128)(2,1)S(1)} collective-permute-done((bf16[384,512]{1,0:T(8,128)(2,1)S(1)}, bf16[384,512]{1,0:T(8,128)(2,1)S(1)}, u32[]{:S(2)}, u32[]{:S(2)}) %collective-permute-start.7) | collective-permute-done | bytes 393248 | tf_op jit(solution)/shard_map/ppermute | solution.py:14
  366.4 0.5 rev.4
  366.9 0.5 fusion.47
  367.4 0.5 copy-done.2
  367.9 0.2 copy-done.3
  368.1 1.4 fusion.48
  (27 shorter events, 0.1 us)
Async XLA Ops:
  6.5 360.4 %copy-start = (bf16[512,512]{1,0:T(8,128)(2,1)S(1)}, bf16[512,512]{1,0:T(8,128)(2,1)}, u32[]{:S(2)}) copy-start(bf16[512,512]{1,0:T(8,128)(2,1)} %param.18) | copy-start | bytes 1572868
  6.5 4.0 %copy-start.4 = (bf16[2,256,512]{2,1,0:T(8,128)(2,1)S(1)}, bf16[2,256,512]{2,1,0:T(8,128)(2,1)}, u32[]{:S(2)}) copy-start(bf16[2,256,512]{2,1,0:T(8,128)(2,1)} %param.15) | copy-start | bytes 1572868
  6.5 6.1 %copy-start.1 = (bf16[1,384,512]{2,1,0:T(8,128)(2,1)S(1)}, bf16[1,384,512]{2,1,0:T(8,128)(2,1)}, u32[]{:S(2)}) copy-start(bf16[1,384,512]{2,1,0:T(8,128)(2,1)} %param.10) | copy-start | bytes 1179652
  6.5 6.2 %copy-start.5 = (f32[2,512]{1,0:T(2,128)S(1)}, f32[2,512]{1,0:T(2,128)}, u32[]{:S(2)}) copy-start(f32[2,512]{1,0:T(2,128)} %param.11) | copy-start | bytes 12292
  6.5 52.5 %all-gather.13.cloned.1.call-start = ((), (), s32[]{:S(2)}) async-start(), calls=%async_computation | async-start | bytes 1769472 | tf_op jit(solution)/shard_map/all_gather | solution.py:44
  8.5 11.3 %copy-start.6 = (f32[2,512]{1,0:T(2,128)S(1)}, f32[2,512]{1,0:T(2,128)}, u32[]{:S(2)}) copy-start(f32[2,512]{1,0:T(2,128)} %param.13) | copy-start | bytes 12292
  8.5 102.5 %all-gather.15.cloned.1.call-start = ((), (), s32[]{:S(2)}) async-start(), calls=%async_computation.1 | async-start | bytes 2359296 | tf_op jit(solution)/shard_map/all_gather | solution.py:50
  10.5 150.2 %all-gather.17.cloned.1.call-start = ((), (), s32[]{:S(2)}) async-start(), calls=%async_computation.2 | async-start | bytes 2359296 | tf_op jit(solution)/shard_map/all_gather | solution.py:53
  11.4 207.2 %all-gather.19.cloned.1.call-start = ((), (), s32[]{:S(2)}) async-start(), calls=%async_computation.3 | async-start | bytes 1769472 | tf_op jit(solution)/shard_map/all_gather | solution.py:44
  12.0 258.4 %all-gather.21.cloned.1.call-start = ((), (), s32[]{:S(2)}) async-start(), calls=%async_computation.4 | async-start | bytes 2359296 | tf_op jit(solution)/shard_map/all_gather | solution.py:50
  12.6 307.3 %all-gather.23.cloned.1.call-start = ((), (), s32[]{:S(2)}) async-start(), calls=%async_computation.5 | async-start | bytes 2359296 | tf_op jit(solution)/shard_map/all_gather | solution.py:53
  13.0 17.6 %collective-permute-start.1 = (bf16[384,512]{1,0:T(8,128)(2,1)S(1)}, bf16[384,512]{1,0:T(8,128)(2,1)S(1)}, u32[]{:S(2)}, u32[]{:S(2)}) collective-permute-start(bf16[384,512]{1,0:T(8,128)(2,1)S(1)} %fusion.57), channel_id=1, source_target_pairs={{4,0},{8,4},{12,8},{5,1},{9,5},{13,9},{6,2},{10,6},{14,10},{7,3},{... | collective-permute-start | bytes 1179656 | tf_op jit(solution)/shard_map/ppermute | solution.py:10
  14.3 47.7 %collective-permute-start = (bf16[384,512]{1,0:T(8,128)(2,1)S(1)}, bf16[384,512]{1,0:T(8,128)(2,1)S(1)}, u32[]{:S(2)}, u32[]{:S(2)}) collective-permute-start(bf16[384,512]{1,0:T(8,128)(2,1)S(1)} %fusion.57), channel_id=1, source_target_pairs={{0,4},{4,8},{8,12},{1,5},{5,9},{9,13},{2,6},{6,10},{10,14},{3,7},{... | collective-permute-start | bytes 1179656 | tf_op jit(solution)/shard_map/ppermute | solution.py:10
  165.2 54.9 %collective-permute-start.3 = (bf16[384,512]{1,0:T(8,128)(2,1)S(1)}, bf16[384,512]{1,0:T(8,128)(2,1)S(1)}, u32[]{:S(2)}, u32[]{:S(2)}) collective-permute-start(bf16[384,512]{1,0:T(8,128)(2,1)S(1)} %multiply_convert_fusion.4), channel_id=1, source_target_pairs={{8,0},{12,4},{9,1},{13,5},{10,2},{14,6},{11,3},{15,7},{24,16},{28,... | collective-permute-start | bytes 1179656 | tf_op jit(solution)/shard_map/ppermute | solution.py:10
  166.5 55.0 %collective-permute-start.2 = (bf16[384,512]{1,0:T(8,128)(2,1)S(1)}, bf16[384,512]{1,0:T(8,128)(2,1)S(1)}, u32[]{:S(2)}, u32[]{:S(2)}) collective-permute-start(bf16[384,512]{1,0:T(8,128)(2,1)S(1)} %multiply_convert_fusion.4), channel_id=1, source_target_pairs={{0,8},{4,12},{1,9},{5,13},{2,10},{6,14},{3,11},{7,15},{16,24},{20,... | collective-permute-start | bytes 1179656 | tf_op jit(solution)/shard_map/ppermute | solution.py:10
  319.9 4.4 %copy-start.7 = (f32[512]{0:T(512)S(1)}, f32[512]{0:T(512)}, u32[]{:S(2)}) copy-start(f32[512]{0:T(512)} %param.16) | copy-start | bytes 6148
  324.4 1.8 collective-permute-start.4
  326.2 11.2 %collective-permute-start.5 = (bf16[384,512]{1,0:T(8,128)(2,1)S(1)}, bf16[384,512]{1,0:T(8,128)(2,1)S(1)}, u32[]{:S(2)}, u32[]{:S(2)}) collective-permute-start(bf16[384,512]{1,0:T(8,128)(2,1)S(1)} %collective-permute-done.4), channel_id=1, source_target_pairs={{0,1},{1,0},{4,5},{5,4},{8,9},{9,8},{12,13},{13,12},{2,3},{3,2},{6... | collective-permute-start | bytes 1179656 | tf_op jit(solution)/shard_map/ppermute | solution.py:14
  337.4 10.3 %collective-permute-start.6 = (bf16[384,512]{1,0:T(8,128)(2,1)S(1)}, bf16[384,512]{1,0:T(8,128)(2,1)S(1)}, u32[]{:S(2)}, u32[]{:S(2)}) collective-permute-start(bf16[384,512]{1,0:T(8,128)(2,1)S(1)} %collective-permute-done.5), channel_id=1, source_target_pairs={{0,4},{1,5},{4,0},{5,1},{8,12},{9,13},{12,8},{13,9},{2,6},{3,7},{6... | collective-permute-start | bytes 1179656 | tf_op jit(solution)/shard_map/ppermute | solution.py:14
  347.7 18.7 %collective-permute-start.7 = (bf16[384,512]{1,0:T(8,128)(2,1)S(1)}, bf16[384,512]{1,0:T(8,128)(2,1)S(1)}, u32[]{:S(2)}, u32[]{:S(2)}) collective-permute-start(bf16[384,512]{1,0:T(8,128)(2,1)S(1)} %collective-permute-done.6), channel_id=1, source_target_pairs={{0,8},{1,9},{4,12},{5,13},{8,0},{9,1},{12,4},{13,5},{2,10},{3,11},... | collective-permute-start | bytes 1179656 | tf_op jit(solution)/shard_map/ppermute | solution.py:14
  366.9 1.0 copy-start.2
  366.9 1.2 copy-start.3
Sparse Core Ops, SparseCore 0:
  9.6 49.4 all-gather.12
  61.1 49.8 all-gather.14
  113.1 47.4 all-gather.16
  162.7 55.8 all-gather.18
  220.5 49.8 all-gather.20
  272.4 47.4 all-gather.22
where the time goes:
time: 377 us; the launch traced here: 376 us
  waiting for transfers between devices  319 us (85%)
  matrix products  19.5 us (5%)
  starting transfers between devices  17.8 us (5%)
  between operations  13.7 us (4%)
  local copies, waits for them, and re-layouts  5.8 us (2%)
    all_gather x2, waiting for transfers between devices, local(): lax.all_gather(down_weight[block], ('seq', 'chan'), axis=0, tiled=True)  99.1 us
    all_gather x2, waiting for transfers between devices, local(): lax.all_gather(up_weight[block], ('seq', 'chan'), axis=1, tiled=True)  94.8 us
    all_gather x2, waiting for transfers between devices, local(): lax.all_gather(conv_weight[block], ('seq', 'chan'), axis=2, tiled=True)  75.1 us
    ppermute x4, waiting for transfers between devices, swapped(): lax.ppermute(x, axis, [(i, i ^ 1 << stride) for i in range(lax.axis_size(...  38.1 us
    dot_general x10, matrix products, matmul(): return jnp.dot(left, right, preferred_element_type=jnp.float32)  19.5 us
    ppermute x4, starting transfers between devices, passed_along(): lax.ppermute(value, axis, [(source, source + steps) for source in range(i...  13.7 us
    ppermute x4, waiting for transfers between devices, passed_along(): lax.ppermute(value, axis, [(source, source + steps) for source in range(i...  10.7 us
  transfers between devices with their start and end apart: 14, of which 11 were waited for; matrix products, arithmetic and copies ran while one was open for 4% of the time, Pallas kernels for 0%

commit v1 on v0

--- a/solution.py
+++ b/solution.py
@@ -2,6 +2,18 @@
 import jax.numpy as jnp
 from jax import lax
 from jax.sharding import PartitionSpec as P
+
+
+def doubled_up(shard, axis, dim):
+    ways, here = (lax.axis_size(axis), lax.axis_index(axis))
+    grown, reach = (shard, 1)
+    while reach < ways:
+        theirs = lax.ppermute(grown, axis, [(d, d ^ reach) for d in range(ways)])
+        mine_first = jnp.concatenate([grown, theirs], axis=dim)
+        theirs_first = jnp.concatenate([theirs, grown], axis=dim)
+        grown = jnp.where(here & reach == 0, mine_first, theirs_first)
+        reach = 2 * reach
+    return grown
 
 
 def passed_along(value, axis, steps):
@@ -47,7 +59,7 @@
         state = state + conv.astype(jnp.float32)
         mixed = normalize(state, ff_norm[block]).astype(jnp.bfloat16)
         hidden = jax.nn.gelu(
-            matmul(mixed, lax.all_gather(up_weight[block], ("seq", "chan"), axis=1, tiled=True))
+            matmul(mixed, doubled_up(up_weight[block], ("seq", "chan"), 1))
         ).astype(jnp.bfloat16)
         state = state + matmul(
             hidden, lax.all_gather(down_weight[block], ("seq", "chan"), axis=0, tiled=True)

time: 377 us -> 336 us (0.89)
  waiting for transfers between devices: 319 us -> 262 us
  starting transfers between devices: 17.8 us -> 27.8 us
  other arithmetic: 0.63 us -> 4.69 us
    all_gather x2 -> x0, waiting for transfers between devices: 94.8 us -> none  [local(): lax.all_gather(up_weight[block], ('seq', 'chan'), axis=1, tiled=True)]
    ppermute x0 -> x6, waiting for transfers between devices: none -> 45.1 us  [doubled_up(): theirs = lax.ppermute(grown, axis, [(d, d ^ reach) for d in range(ways)])]
    ppermute x4, waiting for transfers between devices: 10.7 us -> 34.1 us  [passed_along(): lax.ppermute(value, axis, [(source, source + steps) for source in range(i...]
    all_gather x2, waiting for transfers between devices: 99.1 us -> 79.4 us  [local(): lax.all_gather(down_weight[block], ('seq', 'chan'), axis=0, tiled=True)]
    ppermute x0 -> x6, starting transfers between devices: none -> 13.2 us  [doubled_up(): theirs = lax.ppermute(grown, axis, [(d, d ^ reach) for d in range(ways)])]
    all_gather x2, waiting for transfers between devices: 75.1 us -> 65.1 us  [local(): lax.all_gather(conv_weight[block], ('seq', 'chan'), axis=2, tiled=True)]
  transfers between devices with their start and end apart: 14 -> 18, of which waited for: 11 -> 13; matrix products, arithmetic and copies ran while one was open for 4% -> 7% of each run, Pallas kernels for 0% -> 0%
where the time goes in v1:
time: 336 us; the launch traced here: 335 us
  waiting for transfers between devices  262 us (78%)
  starting transfers between devices  27.8 us (8%)
  matrix products  21.4 us (6%)
  between operations  13.4 us (4%)
  local copies, waits for them, and re-layouts  5.58 us (2%)
  other arithmetic  4.69 us (1%)
    all_gather x2, waiting for transfers between devices, local(): lax.all_gather(down_weight[block], ('seq', 'chan'), axis=0, tiled=True)  79.4 us
    all_gather x2, waiting for transfers between devices, local(): lax.all_gather(conv_weight[block], ('seq', 'chan'), axis=2, tiled=True)  65.1 us
    ppermute x6, waiting for transfers between devices, doubled_up(): theirs = lax.ppermute(grown, axis, [(d, d ^ reach) for d in range(ways)])  45.1 us
    ppermute x4, waiting for transfers between devices, swapped(): lax.ppermute(x, axis, [(i, i ^ 1 << stride) for i in range(lax.axis_size(...  38.1 us
    ppermute x4, waiting for transfers between devices, passed_along(): lax.ppermute(value, axis, [(source, source + steps) for source in range(i...  34.1 us
    dot_general x10, matrix products, matmul(): return jnp.dot(left, right, preferred_element_type=jnp.float32)  21.4 us
    ppermute x6, starting transfers between devices, doubled_up(): theirs = lax.ppermute(grown, axis, [(d, d ^ reach) for d in range(ways)])  13.2 us
    ppermute x4, starting transfers between devices, passed_along(): lax.ppermute(value, axis, [(source, source + steps) for source in range(i...  10.5 us
  transfers between devices with their start and end apart: 18, of which 13 were waited for; matrix products, arithmetic and copies ran while one was open for 7% of the time, Pallas kernels for 0%

profile of v1, /device:TPU:0, one launch (start us, length us, event | category | flops | bytes accessed | tf_op | source)
XLA Modules:
  0.0 335.3 jit_solution(11896056782516662570)
XLA Ops:
  6.6 1.9 fusion.91
  8.6 1.9 fusion.90
  10.6 0.7 all-gather.13.cloned.1.call-update
  11.4 3.0 collective-permute-start.2
  14.4 0.2 fusion.57
  14.6 6.9 %collective-permute-done.2 = bf16[512,256]{1,0:T(8,128)(2,1)S(1)} collective-permute-done((bf16[512,256]{1,0:T(8,128)(2,1)S(1)}, bf16[512,256]{1,0:T(8,128)(2,1)S(1)}, u32[]{:S(2)}, u32[]{:S(2)}) %collective-permute-start.2) | collective-permute-done | bytes 262176 | tf_op jit(solution)/shard_map/ppermute | solution.py:11
  21.6 2.2 collective-permute-start.3
  23.8 0.9 fusion.59
  24.7 1.3 collective-permute-start.1
  26.0 5.3 %collective-permute-start = (bf16[384,512]{1,0:T(8,128)(2,1)}, bf16[384,512]{1,0:T(8,128)(2,1)}, u32[]{:S(2)}, u32[]{:S(2)}) collective-permute-start(bf16[384,512]{1,0:T(8,128)(2,1)} %fusion.59), channel_id=1, source_target_pairs={{0,4},{4,8},{8,12},{1,5},{5,9},{9,13},{2,6},{6,10},{10,14},{3,7},{... | collective-permute-start | bytes 1179656 | tf_op jit(solution)/shard_map/ppermute | solution.py:22
  31.4 0.5 fusion.92
  32.0 0.5 collective-permute-start.8
  32.5 8.6 %collective-permute-done.3 = bf16[512,512]{1,0:T(8,128)(2,1)} collective-permute-done((bf16[512,512]{1,0:T(8,128)(2,1)S(1)}, bf16[512,512]{1,0:T(8,128)(2,1)}, u32[]{:S(2)}, u32[]{:S(2)}) %collective-permute-start.3) | collective-permute-done | bytes 524320 | tf_op jit(solution)/shard_map/ppermute | solution.py:11
  41.1 1.5 maximum_select_fusion.8
  42.6 3.1 collective-permute-start.4
  45.7 34.1 %collective-permute-done.1 = bf16[384,512]{1,0:T(8,128)(2,1)} collective-permute-done((bf16[384,512]{1,0:T(8,128)(2,1)}, bf16[384,512]{1,0:T(8,128)(2,1)}, u32[]{:S(2)}, u32[]{:S(2)}) %collective-permute-start.1) | collective-permute-done | bytes 393248 | tf_op jit(solution)/shard_map/ppermute | solution.py:22
  79.8 0.2 all-gather.9.cloned.1.call-done
  80.0 1.6 fusion.64
  81.6 1.5 fusion.65
  83.1 2.6 multiply_reduce_fusion.3
  85.7 24.1 %collective-permute-done.4 = bf16[512,1024]{1,0:T(8,128)(2,1)} collective-permute-done((bf16[512,1024]{1,0:T(8,128)(2,1)S(1)}, bf16[512,1024]{1,0:T(8,128)(2,1)}, u32[]{:S(2)}, u32[]{:S(2)}) %collective-permute-start.4) | collective-permute-done | bytes 1048608 | tf_op jit(solution)/shard_map/ppermute | solution.py:11
  109.7 27.2 %all-gather.11.cloned.1.call-done = bf16[1,2048,512]{2,1,0:T(8,128)(2,1)} async-done(((bf16[1,256,512]{2,1,0:T(8,128)(2,1)}), bf16[1,2048,512]{2,1,0:T(8,128)(2,1)}) %all-gather.11.cloned.1.call-update) | async-done | bytes 2097168 | tf_op jit(solution)/shard_map/all_gather | solution.py:65
  137.0 4.9 %multiply_reduce_fusion.2 = (f32[384]{0:T(512)S(1)}, f32[384,512]{1,0:T(8,128)S(1)}) fusion(f32[384,512]{1,0:T(8,128)} %get-tuple-element.16, bf16[1,2048,512]{2,1,0:T(8,128)(2,1)} %all-gather.11.cloned.1.call-done, bf16[512,1024]{1,0:T(8,128)(2,1)} %collective-permute-done.4, bf16[512,1024]{1,0:T(8,128)(2,1)S(1)} %maximum_select_fusion.8, pred[]{:T(512)S(6)} %eq.12, ...), kind=kOutput, calls=%fused_computation.76 | convolution fusion | flops 1628307072 | bytes 5772289 | tf_op jit(solution)/shard_map/dot_general | solution.py:34
  141.9 0.1 multiply_convert_fusion.4
  142.0 1.3 collective-permute-start.6
  143.3 1.5 maximum_select_fusion.9
  144.9 4.4 %collective-permute-start.9 = (bf16[512,1024]{1,0:T(8,128)(2,1)S(1)}, bf16[512,1024]{1,0:T(8,128)(2,1)}, u32[]{:S(2)}, u32[]{:S(2)}) collective-permute-start(bf16[512,1024]{1,0:T(8,128)(2,1)S(1)} %maximum_select_fusion.9), channel_id=1, source_target_pairs={{0,8},{1,9},{4,12},{5,13},{8,0},{9,1},{12,4},{13,5},{2,10},{3,11},... | collective-permute-start | bytes 3145736 | tf_op jit(solution)/shard_map/ppermute | solution.py:11
  149.2 2.7 collective-permute-start.5
  151.9 64.8 %all-gather.13.cloned.1.call-done = bf16[1,3,512,512]{2,3,1,0:T(8,128)(2,1)} async-done(((bf16[1,3,512,64]{2,3,1,0:T(8,128)(2,1)}), bf16[1,3,512,512]{2,3,1,0:T(8,128)(2,1)}) %all-gather.13.cloned.1.call-update) | async-done | bytes 1572880 | tf_op jit(solution)/shard_map/all_gather | solution.py:56
  216.8 1.4 fusion.63
  218.2 1.6 fusion.62
  219.8 1.7 multiply_reduce_fusion.1
  221.5 5.6 %collective-permute-done.9 = bf16[512,1024]{1,0:T(8,128)(2,1)} collective-permute-done((bf16[512,1024]{1,0:T(8,128)(2,1)S(1)}, bf16[512,1024]{1,0:T(8,128)(2,1)}, u32[]{:S(2)}, u32[]{:S(2)}) %collective-permute-start.9) | collective-permute-done | bytes 1048608 | tf_op jit(solution)/shard_map/ppermute | solution.py:11
  227.0 52.2 %all-gather.15.cloned.1.call-done = bf16[1,2048,512]{2,1,0:T(8,128)(2,1)} async-done(((bf16[1,256,512]{2,1,0:T(8,128)(2,1)}), bf16[1,2048,512]{2,1,0:T(8,128)(2,1)}) %all-gather.15.cloned.1.call-update) | async-done | bytes 2097168 | tf_op jit(solution)/shard_map/all_gather | solution.py:65
  279.2 4.4 %multiply_reduce_fusion = (f32[384]{0:T(512)S(1)}, f32[384,512]{1,0:T(8,128)S(1)}) fusion(f32[384,512]{1,0:T(8,128)S(1)} %get-tuple-element.20, bf16[1,2048,512]{2,1,0:T(8,128)(2,1)} %all-gather.15.cloned.1.call-done, bf16[512,1024]{1,0:T(8,128)(2,1)} %collective-permute-done.9, bf16[512,1024]{1,0:T(8,128)(2,1)S(1)} %maximum_select_fusion.9, pred[]{:T(512)S(6)} %eq.12, ...), kind=kOutput, calls=%fused_computation.72 | convolution fusion | flops 1628307072 | bytes 5772289 | tf_op jit(solution)/shard_map/dot_general | solution.py:34
  283.6 0.1 multiply_convert_fusion
  283.8 1.7 collective-permute-done.10
  285.5 0.6 collective-permute-start.11
  286.1 10.6 %collective-permute-done.11 = bf16[384,512]{1,0:T(8,128)(2,1)S(1)} collective-permute-done((bf16[384,512]{1,0:T(8,128)(2,1)S(1)}, bf16[384,512]{1,0:T(8,128)(2,1)S(1)}, u32[]{:S(2)}, u32[]{:S(2)}) %collective-permute-start.11) | collective-permute-done | bytes 393248 | tf_op jit(solution)/shard_map/ppermute | solution.py:26
  296.7 1.5 collective-permute-start.12
  298.2 8.8 %collective-permute-done.12 = bf16[384,512]{1,0:T(8,128)(2,1)S(1)} collective-permute-done((bf16[384,512]{1,0:T(8,128)(2,1)S(1)}, bf16[384,512]{1,0:T(8,128)(2,1)S(1)}, u32[]{:S(2)}, u32[]{:S(2)}) %collective-permute-start.12) | collective-permute-done | bytes 393248 | tf_op jit(solution)/shard_map/ppermute | solution.py:26
  307.0 1.8 collective-permute-start.13
  308.8 16.9 %collective-permute-done.13 = bf16[384,512]{1,0:T(8,128)(2,1)S(1)} collective-permute-done((bf16[384,512]{1,0:T(8,128)(2,1)S(1)}, bf16[384,512]{1,0:T(8,128)(2,1)S(1)}, u32[]{:S(2)}, u32[]{:S(2)}) %collective-permute-start.13) | collective-permute-done | bytes 393248 | tf_op jit(solution)/shard_map/ppermute | solution.py:26
  325.8 0.5 rev.4
  326.3 0.5 fusion.53
  326.7 0.5 copy-done.2
  327.3 0.2 copy-done.3
  327.4 1.4 fusion.54
  (39 shorter events, 0.7 us)
Async XLA Ops:
  6.5 319.7 %copy-start = (bf16[512,512]{1,0:T(8,128)(2,1)S(1)}, bf16[512,512]{1,0:T(8,128)(2,1)}, u32[]{:S(2)}) copy-start(bf16[512,512]{1,0:T(8,128)(2,1)} %param.18) | copy-start | bytes 1572868
  6.5 4.8 %copy-start.4 = (bf16[2,512,256]{2,1,0:T(8,128)(2,1)S(1)}, bf16[2,512,256]{2,1,0:T(8,128)(2,1)}, u32[]{:S(2)}) copy-start(bf16[2,512,256]{2,1,0:T(8,128)(2,1)} %param.14) | copy-start | bytes 1572868
  6.5 7.9 %copy-start.1 = (bf16[1,384,512]{2,1,0:T(8,128)(2,1)S(1)}, bf16[1,384,512]{2,1,0:T(8,128)(2,1)}, u32[]{:S(2)}) copy-start(bf16[1,384,512]{2,1,0:T(8,128)(2,1)} %param.10) | copy-start | bytes 1179652
  6.5 8.1 %copy-start.5 = (f32[2,512]{1,0:T(2,128)S(1)}, f32[2,512]{1,0:T(2,128)}, u32[]{:S(2)}) copy-start(f32[2,512]{1,0:T(2,128)} %param.11) | copy-start | bytes 12292
  6.5 73.5 %all-gather.9.cloned.1.call-start = ((), (), s32[]{:S(2)}) async-start(), calls=%async_computation | async-start | bytes 1769472 | tf_op jit(solution)/shard_map/all_gather | solution.py:56
  8.6 128.4 %all-gather.11.cloned.1.call-start = ((), (), s32[]{:S(2)}) async-start(), calls=%async_computation.1 | async-start | bytes 2359296 | tf_op jit(solution)/shard_map/all_gather | solution.py:65
  10.5 20.9 %copy-start.6 = (f32[2,512]{1,0:T(2,128)S(1)}, f32[2,512]{1,0:T(2,128)}, u32[]{:S(2)}) copy-start(f32[2,512]{1,0:T(2,128)} %param.13) | copy-start | bytes 12292
  10.5 206.2 %all-gather.13.cloned.1.call-start = ((), (), s32[]{:S(2)}) async-start(), calls=%async_computation.2 | async-start | bytes 1769472 | tf_op jit(solution)/shard_map/all_gather | solution.py:56
  11.3 267.9 %all-gather.15.cloned.1.call-start = ((), (), s32[]{:S(2)}) async-start(), calls=%async_computation.3 | async-start | bytes 2359296 | tf_op jit(solution)/shard_map/all_gather | solution.py:65
  11.4 10.1 %collective-permute-start.2 = (bf16[512,256]{1,0:T(8,128)(2,1)S(1)}, bf16[512,256]{1,0:T(8,128)(2,1)S(1)}, u32[]{:S(2)}, u32[]{:S(2)}) collective-permute-start(bf16[512,256]{1,0:T(8,128)(2,1)S(1)} %get-tuple-element.6), channel_id=1, source_target_pairs={{0,1},{1,0},{4,5},{5,4},{8,9},{9,8},{12,13},{13,12},{2,3},{3,2},{6... | collective-permute-start | bytes 786440 | tf_op jit(solution)/shard_map/ppermute | solution.py:11
  14.4 17.5 %collective-permute-start.7 = (bf16[512,256]{1,0:T(8,128)(2,1)S(1)}, bf16[512,256]{1,0:T(8,128)(2,1)S(1)}, u32[]{:S(2)}, u32[]{:S(2)}) collective-permute-start(bf16[512,256]{1,0:T(8,128)(2,1)S(1)} %get-tuple-element.5), channel_id=1, source_target_pairs={{0,1},{1,0},{4,5},{5,4},{8,9},{9,8},{12,13},{13,12},{2,3},{3,2},{6... | collective-permute-start | bytes 786440 | tf_op jit(solution)/shard_map/ppermute | solution.py:11
  21.6 19.5 %collective-permute-start.3 = (bf16[512,512]{1,0:T(8,128)(2,1)S(1)}, bf16[512,512]{1,0:T(8,128)(2,1)}, u32[]{:S(2)}, u32[]{:S(2)}) collective-permute-start(bf16[512,512]{1,0:T(8,128)(2,1)S(1)} %maximum_select_fusion.14), channel_id=1, source_target_pairs={{0,4},{1,5},{4,0},{5,1},{8,12},{9,13},{12,8},{13,9},{2,6},{3,7},{6... | collective-permute-start | bytes 1572872 | tf_op jit(solution)/shard_map/ppermute | solution.py:11
  24.7 55.0 %collective-permute-start.1 = (bf16[384,512]{1,0:T(8,128)(2,1)}, bf16[384,512]{1,0:T(8,128)(2,1)}, u32[]{:S(2)}, u32[]{:S(2)}) collective-permute-start(bf16[384,512]{1,0:T(8,128)(2,1)} %fusion.59), channel_id=1, source_target_pairs={{4,0},{8,4},{12,8},{5,1},{9,5},{13,9},{6,2},{10,6},{14,10},{7,3},{... | collective-permute-start | bytes 1179656 | tf_op jit(solution)/shard_map/ppermute | solution.py:22
  26.0 57.0 %collective-permute-start = (bf16[384,512]{1,0:T(8,128)(2,1)}, bf16[384,512]{1,0:T(8,128)(2,1)}, u32[]{:S(2)}, u32[]{:S(2)}) collective-permute-start(bf16[384,512]{1,0:T(8,128)(2,1)} %fusion.59), channel_id=1, source_target_pairs={{0,4},{4,8},{8,12},{1,5},{5,9},{9,13},{2,6},{6,10},{10,14},{3,7},{... | collective-permute-start | bytes 1179656 | tf_op jit(solution)/shard_map/ppermute | solution.py:22
  32.0 111.3 %collective-permute-start.8 = (bf16[512,512]{1,0:T(8,128)(2,1)S(1)}, bf16[512,512]{1,0:T(8,128)(2,1)}, u32[]{:S(2)}, u32[]{:S(2)}) collective-permute-start(bf16[512,512]{1,0:T(8,128)(2,1)S(1)} %maximum_select_fusion.15), channel_id=1, source_target_pairs={{0,4},{1,5},{4,0},{5,1},{8,12},{9,13},{12,8},{13,9},{2,6},{3,7},{6... | collective-permute-start | bytes 1572872 | tf_op jit(solution)/shard_map/ppermute | solution.py:11
  42.6 67.1 %collective-permute-start.4 = (bf16[512,1024]{1,0:T(8,128)(2,1)S(1)}, bf16[512,1024]{1,0:T(8,128)(2,1)}, u32[]{:S(2)}, u32[]{:S(2)}) collective-permute-start(bf16[512,1024]{1,0:T(8,128)(2,1)S(1)} %maximum_select_fusion.8), channel_id=1, source_target_pairs={{0,8},{1,9},{4,12},{5,13},{8,0},{9,1},{12,4},{13,5},{2,10},{3,11},... | collective-permute-start | bytes 3145736 | tf_op jit(solution)/shard_map/ppermute | solution.py:11
  83.0 53.9 %copy-start.8 = (f32[1,512]{1,0:T(1,128)S(1)}, f32[1,512]{1,0:T(1,128)}, u32[]{:S(2)}) copy-start(f32[1,512]{1,0:T(1,128)} %get-tuple-element.12) | copy-start | bytes 6148
  142.0 76.2 %collective-permute-start.6 = (bf16[384,512]{1,0:T(8,128)(2,1)S(1)}, bf16[384,512]{1,0:T(8,128)(2,1)}, u32[]{:S(2)}, u32[]{:S(2)}) collective-permute-start(bf16[384,512]{1,0:T(8,128)(2,1)S(1)} %multiply_convert_fusion.4), channel_id=1, source_target_pairs={{8,0},{12,4},{9,1},{13,5},{10,2},{14,6},{11,3},{15,7},{24,16},{28,... | collective-permute-start | bytes 1179656 | tf_op jit(solution)/shard_map/ppermute | solution.py:22
  144.9 82.2 %collective-permute-start.9 = (bf16[512,1024]{1,0:T(8,128)(2,1)S(1)}, bf16[512,1024]{1,0:T(8,128)(2,1)}, u32[]{:S(2)}, u32[]{:S(2)}) collective-permute-start(bf16[512,1024]{1,0:T(8,128)(2,1)S(1)} %maximum_select_fusion.9), channel_id=1, source_target_pairs={{0,8},{1,9},{4,12},{5,13},{8,0},{9,1},{12,4},{13,5},{2,10},{3,11},... | collective-permute-start | bytes 3145736 | tf_op jit(solution)/shard_map/ppermute | solution.py:11
  149.2 70.5 %collective-permute-start.5 = (bf16[384,512]{1,0:T(8,128)(2,1)S(1)}, bf16[384,512]{1,0:T(8,128)(2,1)}, u32[]{:S(2)}, u32[]{:S(2)}) collective-permute-start(bf16[384,512]{1,0:T(8,128)(2,1)S(1)} %multiply_convert_fusion.4), channel_id=1, source_target_pairs={{0,8},{4,12},{1,9},{5,13},{2,10},{6,14},{3,11},{7,15},{16,24},{20,... | collective-permute-start | bytes 1179656 | tf_op jit(solution)/shard_map/ppermute | solution.py:22
  279.2 4.4 %copy-start.7 = (f32[512]{0:T(512)S(1)}, f32[512]{0:T(512)}, u32[]{:S(2)}) copy-start(f32[512]{0:T(512)} %param.16) | copy-start | bytes 6148
  283.8 1.8 collective-permute-start.10
  285.5 11.2 %collective-permute-start.11 = (bf16[384,512]{1,0:T(8,128)(2,1)S(1)}, bf16[384,512]{1,0:T(8,128)(2,1)S(1)}, u32[]{:S(2)}, u32[]{:S(2)}) collective-permute-start(bf16[384,512]{1,0:T(8,128)(2,1)S(1)} %collective-permute-done.10), channel_id=1, source_target_pairs={{0,1},{1,0},{4,5},{5,4},{8,9},{9,8},{12,13},{13,12},{2,3},{3,2},{6... | collective-permute-start | bytes 1179656 | tf_op jit(solution)/shard_map/ppermute | solution.py:26
  296.7 10.3 %collective-permute-start.12 = (bf16[384,512]{1,0:T(8,128)(2,1)S(1)}, bf16[384,512]{1,0:T(8,128)(2,1)S(1)}, u32[]{:S(2)}, u32[]{:S(2)}) collective-permute-start(bf16[384,512]{1,0:T(8,128)(2,1)S(1)} %collective-permute-done.11), channel_id=1, source_target_pairs={{0,4},{1,5},{4,0},{5,1},{8,12},{9,13},{12,8},{13,9},{2,6},{3,7},{6... | collective-permute-start | bytes 1179656 | tf_op jit(solution)/shard_map/ppermute | solution.py:26
  307.0 18.7 %collective-permute-start.13 = (bf16[384,512]{1,0:T(8,128)(2,1)S(1)}, bf16[384,512]{1,0:T(8,128)(2,1)S(1)}, u32[]{:S(2)}, u32[]{:S(2)}) collective-permute-start(bf16[384,512]{1,0:T(8,128)(2,1)S(1)} %collective-permute-done.12), channel_id=1, source_target_pairs={{0,8},{1,9},{4,12},{5,13},{8,0},{9,1},{12,4},{13,5},{2,10},{3,11},... | collective-permute-start | bytes 1179656 | tf_op jit(solution)/shard_map/ppermute | solution.py:26
  326.2 1.0 copy-start.2
  326.2 1.2 copy-start.3
Sparse Core Ops, SparseCore 0:
  9.6 70.4 all-gather.8
  82.1 54.7 all-gather.10
  139.2 77.5 all-gather.12
  218.7 60.4 all-gather.14
